TPU v7x, 512 devices: a whole 4x8x8 slice. The times are simulated.
512 devices in a mesh: dp: 64 (over y, z_lo, core), tensor: 8 (over z_hi, x).
Axes of the slice: x: 4, y: 8, z: 8 (z_hi: 2, z_lo: 4; z = z_hi * 4 + z_lo), core: 2. Of those that a mesh axis runs over, the one named last changes fastest.
Arguments:
- layer_input: bfloat16 [2, 4096, 8192], P(None, ('dp', 'tensor')), may hold values from -6 to 6
- key_gradient_rows: bfloat16 [2, 4096, 1024], P(None, 'dp', 'tensor'), may hold values from -6 to 6
- key_block_matrix: bfloat16 [8, 6144, 128], P('tensor', 'dp'), may hold values from -0.09375 to 0.09375
- kept_rows: int32 [8, 48], replicated, may hold values from -1 to 63, as said below
Outputs:
- weight_grad: float32 [8, 6144, 128], P('tensor', 'dp')
- input_grad: bfloat16 [2, 4096, 8192], P(None, ('dp', 'tensor'))
Inputs may be any that keep to these rules, and one draw needn't show every extreme that they name: `kept_rows`: row h lists in ascending order the distinct blocks (of the 64 blocks of 128 input rows) that survive pruning for head h, then -1 in its unused slots. At most 48 blocks survive for one head and exactly 48 for some head; 256 blocks survive in all, at least one for every head.
All inputs are finite; a program needn't handle non-finite values.
Results may differ from a plain program's by a relative error of at most 0.005.
Values may be sent and summed in bfloat16 or wider, within the bound.
A program may use at most 64 MiB of HBM per device.

v0:
```python
import math
import jax
import jax.numpy as jnp
from jax import lax
from jax.sharding import PartitionSpec as P

MODEL_WIDTH = 8192
HEAD_WIDTH = 128
PRUNE_BLOCK_ROWS = 128
HEAD_BLOCK_LIMIT = 48
MICRO_BATCHES = 2


def local(layer_input, key_gradient_rows, key_block_matrix, kept_rows):
    my_head = lax.axis_index("tensor")
    groups = lax.axis_size("tensor")
    block_count = MODEL_WIDTH // PRUNE_BLOCK_ROWS
    own_rows = lax.dynamic_index_in_dim(kept_rows, my_head, 0, keepdims=False)
    alive = own_rows >= 0
    clipped = jnp.maximum(own_rows, 0)
    gathered_w = lax.all_gather(key_block_matrix, "dp", axis=1, tiled=True)
    blocks_w = gathered_w.reshape(HEAD_BLOCK_LIMIT, PRUNE_BLOCK_ROWS, HEAD_WIDTH) * alive[
        :, None, None
    ].astype(jnp.bfloat16)
    placing = (kept_rows[:, :, None] == jnp.arange(block_count)[None, None, :]).astype(jnp.bfloat16)
    accum = jnp.zeros((HEAD_BLOCK_LIMIT, PRUNE_BLOCK_ROWS, HEAD_WIDTH), jnp.float32)
    results = []
    for micro in range(MICRO_BATCHES):
        grads_here = key_gradient_rows[micro]
        group_x = lax.all_gather(layer_input[micro], "tensor", axis=0, tiled=True)
        picked = jnp.take(
            group_x.reshape(group_x.shape[0], block_count, PRUNE_BLOCK_ROWS), clipped, axis=1
        )
        product = jnp.einsum("gcb,gh->cbh", picked, grads_here, preferred_element_type=jnp.float32)
        accum = accum + product * alive[:, None, None].astype(jnp.float32)
        partial_value = jnp.einsum(
            "gh,cbh->gcb", grads_here, blocks_w, preferred_element_type=jnp.float32
        ).astype(jnp.bfloat16)
        partial_value = partial_value.reshape(
            grads_here.shape[0], 1, HEAD_BLOCK_LIMIT * PRUNE_BLOCK_ROWS
        )
        received = lax.all_to_all(partial_value, "tensor", split_axis=0, concat_axis=1, tiled=True)
        own_tokens = received.shape[0]
        received = received.reshape(own_tokens, groups, HEAD_BLOCK_LIMIT, PRUNE_BLOCK_ROWS)
        summed = jnp.einsum("tkcb,kcn->tnb", received, placing, preferred_element_type=jnp.float32)
        results.append(summed.reshape(own_tokens, MODEL_WIDTH).astype(jnp.bfloat16))
    owned = lax.psum_scatter(
        accum.reshape(HEAD_BLOCK_LIMIT * PRUNE_BLOCK_ROWS, HEAD_WIDTH),
        "dp",
        scatter_dimension=0,
        tiled=True,
    )
    scale = 1.0 / math.sqrt(MICRO_BATCHES * key_gradient_rows.shape[1] * lax.axis_size("dp"))
    weight_grad = (owned * scale)[None, :, :]
    return (weight_grad, jnp.stack(results))


def solution(mesh):
    placed = (
        P(None, ("dp", "tensor"), None),
        P(None, "dp", "tensor"),
        P("tensor", "dp", None),
        P(),
    )
    return jax.shard_map(
        local,
        mesh=mesh,
        in_specs=placed,
        out_specs=(P("tensor", "dp", None), P(None, ("dp", "tensor"), None)),
        check_vma=False,
    )
```

profile of v0, /device:TPU:6, one launch (start us, length us, event | category | flops | bytes accessed | tf_op | source)
XLA Modules:
  0.0 561.7 jit_solution(8836301085394832991)
XLA Ops:
  7.2 1.7 fusion.36
  9.0 0.7 all-gather.8.cloned.1.call-update
  10.4 0.7 fusion.32
  11.1 0.7 compare_and_fusion
  11.8 72.0 %all-gather.10.cloned.1.call-done = bf16[1,64,8192]{2,1,0:T(8,128)(2,1)} async-done(((bf16[1,8,8192]{2,1,0:T(8,128)(2,1)}), bf16[1,64,8192]{2,1,0:T(8,128)(2,1)}) %all-gather.10.cloned.1.call-update) | async-done | bytes 1048592 | tf_op jit(solution)/shard_map/all_gather | solution.py:30
  83.8 1.5 copy.31
  85.3 0.7 copy.17
  86.0 64.4 %all-gather.8.cloned.1.call-done = bf16[1,64,8192]{2,1,0:T(8,128)(2,1)} async-done(((bf16[1,8,8192]{2,1,0:T(8,128)(2,1)}), bf16[1,64,8192]{2,1,0:T(8,128)(2,1)}) %all-gather.8.cloned.1.call-update) | async-done | bytes 1048592 | tf_op jit(solution)/shard_map/all_gather | solution.py:30
  150.5 1.5 copy.30
  152.7 0.7 gather_fusion.1
  153.4 0.7 gather_fusion
  154.1 0.8 fusion.11
  154.9 2.8 add_multiply_fusion
  157.8 109.0 %all-gather.6.cloned.1.call-done = bf16[1,6144,128]{2,1,0:T(8,128)(2,1)} async-done(((bf16[1,96,128]{2,1,0:T(8,128)(2,1)}), bf16[1,6144,128]{2,1,0:T(8,128)(2,1)}) %all-gather.6.cloned.1.call-update) | async-done | bytes 1572880 | tf_op jit(solution)/shard_map/all_gather | solution.py:21
  266.8 2.1 broadcast_multiply_fusion
  269.6 1.4 copy.21
  271.0 4.4 reshape.124
  275.9 6.2 %reduce = bf16[64,6144]{1,0:T(8,128)(2,1)} reduce(bf16[64,1,6144]{2,1,0:T(2,128)(2,1)S(1)} %reshape.124, bf16[]{:T(256)} %broadcast.58), dimensions={1}, to_apply=%reshape.124.reduce_sub_computation | reduce | bytes 1572866 | tf_op jit(solution)/shard_map/reshape | solution.py:39
  282.2 3.2 reshape.126
  285.3 8.2 %all-to-all-start.1 = ((bf16[8,2,24576]{2,1,0:T(2,128)(2,1)}), bf16[8,2,24576]{2,1,0:T(2,128)(2,1)S(1)}, u32[]{:S(2)}, u32[]{:S(2)}) async-start(bf16[8,2,24576]{2,1,0:T(2,128)(2,1)} %reshape.126), calls=%async_computation.2 | async-start | bytes 1572864 | tf_op jit(solution)/shard_map/all_to_all | solution.py:42
  294.2 1.4 copy.18
  295.6 4.4 reshape.122
  300.1 5.4 reduce.1
  305.4 1.7 reshape.128
  307.1 5.2 all-to-all-done.1
  312.3 4.9 all-to-all-start
  317.2 0.8 reshape.127
  319.2 13.0 %all-to-all-done = bf16[8,2,24576]{2,1,0:T(2,128)(2,1)S(1)} async-done(((bf16[8,2,24576]{2,1,0:T(2,128)(2,1)}), bf16[8,2,24576]{2,1,0:T(2,128)(2,1)S(1)}, u32[]{:S(2)}, u32[]{:S(2)}) %all-to-all-start) | async-done | bytes 786464 | tf_op jit(solution)/shard_map/all_to_all | solution.py:42
  332.2 0.8 reshape.129
  334.0 0.7 pad_maximum_fusion
  334.7 219.0 %reduce-scatter.2.cloned.1.call-done = f32[96,128]{1,0:T(8,128)} async-done(((f32[6144,128]{1,0:T(8,128)}), f32[96,128]{1,0:T(8,128)}) %reduce-scatter.2.cloned.1.call-update) | async-done | bytes 49168 | tf_op jit(solution)/shard_map/reduce_scatter | solution.py:47
  553.7 1.4 multiply_bitcast_fusion
  (23 shorter events, 5.6 us)
Async XLA Ops:
  7.2 76.7 %all-gather.10.cloned.1.call-start = ((), (), s32[]{:S(2)}) async-start(), calls=%async_computation.6 | async-start | bytes 1179648 | tf_op jit(solution)/shard_map/all_gather | solution.py:30
  8.9 141.6 %all-gather.8.cloned.1.call-start = ((), (), s32[]{:S(2)}) async-start(), calls=%async_computation.5 | async-start | bytes 1179648 | tf_op jit(solution)/shard_map/all_gather | solution.py:30
  9.7 257.1 %all-gather.6.cloned.1.call-start = ((), (), s32[]{:S(2)}) async-start(), calls=%async_computation.4 | async-start | bytes 1597440 | tf_op jit(solution)/shard_map/all_gather | solution.py:21
  10.4 543.3 %reduce-scatter.2.cloned.1.call-start = ((), (), s32[]{:S(2)}) async-start(), calls=%async_computation.3 | async-start | bytes 3194880 | tf_op jit(solution)/shard_map/reduce_scatter | solution.py:47
  152.7 1.4 copy-start
  285.3 27.0 %all-to-all-start.1 = ((bf16[8,2,24576]{2,1,0:T(2,128)(2,1)}), bf16[8,2,24576]{2,1,0:T(2,128)(2,1)S(1)}, u32[]{:S(2)}, u32[]{:S(2)}) async-start(bf16[8,2,24576]{2,1,0:T(2,128)(2,1)} %reshape.126), calls=%async_computation.2 | async-start | bytes 1572864 | tf_op jit(solution)/shard_map/all_to_all | solution.py:42
  312.3 19.9 %all-to-all-start = ((bf16[8,2,24576]{2,1,0:T(2,128)(2,1)}), bf16[8,2,24576]{2,1,0:T(2,128)(2,1)S(1)}, u32[]{:S(2)}, u32[]{:S(2)}) async-start(bf16[8,2,24576]{2,1,0:T(2,128)(2,1)} %reshape.128), calls=%async_computation.1 | async-start | bytes 1572864 | tf_op jit(solution)/shard_map/all_to_all | solution.py:42
  318.0 0.7 copy-start.1
Sparse Core Ops, SparseCore 0:
  11.8 72.0 all-gather.9
  87.0 63.3 all-gather.7
  152.6 114.1 all-gather.5
  269.4 284.2 reduce-scatter.1
where the time goes:
time: 562 us
  waiting for transfers between devices  484 us (86%)
  local copies, waits for them, and re-layouts  27.4 us (5%)
  other arithmetic  17.2 us (3%)
  between operations  14 us (2%)
  starting transfers between devices  13.3 us (2%)
  matrix products  5.81 us (1%)
    reduce_scatter x1, waiting for transfers between devices, local(): lax.psum_scatter(accum.reshape(HEAD_BLOCK_LIMIT * PRUNE_BLOCK_ROWS, HEAD_...  219 us
    all_gather x2, waiting for transfers between devices, local(): group_x = lax.all_gather(layer_input[micro], 'tensor', axis=0, tiled=True)  136 us
    all_gather x1, waiting for transfers between devices, local(): gathered_w = lax.all_gather(key_block_matrix, 'dp', axis=1, tiled=True)  109 us
    all_to_all x2, waiting for transfers between devices, local(): lax.all_to_all(partial_value, 'tensor', split_axis=0, concat_axis=1, tile...  18.1 us
    all_to_all x2, starting transfers between devices, local(): lax.all_to_all(partial_value, 'tensor', split_axis=0, concat_axis=1, tile...  13.1 us
    reshape x2, other arithmetic, local(): partial_value.reshape(grads_here.shape[0], 1, HEAD_BLOCK_LIMIT * PRUNE_BL...  11.6 us
  transfers between devices with their start and end apart: 6, of which 6 were waited for; matrix products, arithmetic and copies ran while one was open for 8% of the time, Pallas kernels for 0%

commit v1 on v0

--- a/solution.py
+++ b/solution.py
@@ -27,7 +27,9 @@
     results = []
     for micro in range(MICRO_BATCHES):
         grads_here = key_gradient_rows[micro]
-        group_x = lax.all_gather(layer_input[micro], "tensor", axis=0, tiled=True)
+        block = layer_input[micro]
+        sent = jnp.stack([block] * lax.axis_size("tensor"))
+        group_x = jnp.concatenate(lax.all_to_all(sent, "tensor", 0, 0), axis=0)
         picked = jnp.take(
             group_x.reshape(group_x.shape[0], block_count, PRUNE_BLOCK_ROWS), clipped, axis=1
         )

time: 562 us -> 462 us (0.82)
  waiting for transfers between devices: 484 us -> 353 us
  starting transfers between devices: 13.3 us -> 46.4 us
    all_gather x2 -> x0, waiting for transfers between devices: 136 us -> none  [local(): group_x = lax.all_gather(layer_input[micro], 'tensor', axis=0, tiled=True)]
    all_to_all x0 -> x2, waiting for transfers between devices: none -> 29.1 us  [local(): group_x = jnp.concatenate(lax.all_to_all(sent, 'tensor', 0, 0), axis=0)]
    all_to_all x0 -> x2, starting transfers between devices: none -> 28.5 us  [local(): group_x = jnp.concatenate(lax.all_to_all(sent, 'tensor', 0, 0), axis=0)]
    all_gather x1, waiting for transfers between devices: 109 us -> 84.5 us  [local(): gathered_w = lax.all_gather(key_block_matrix, 'dp', axis=1, tiled=True)]
    all_to_all x2, waiting for transfers between devices: 18.1 us -> 32.8 us  [local(): lax.all_to_all(partial_value, 'tensor', split_axis=0, concat_axis=1, tile...]
    reduce_scatter x1, waiting for transfers between devices: 219 us -> 206 us  [local(): lax.psum_scatter(accum.reshape(HEAD_BLOCK_LIMIT * PRUNE_BLOCK_ROWS, HEAD_...]
  transfers between devices with their start and end apart: 6 -> 6, of which waited for: 6 -> 6; matrix products, arithmetic and copies ran while one was open for 8% -> 10% of each run, Pallas kernels for 0% -> 0%
where the time goes in v1:
time: 462 us; the launch traced here: 461 us
  waiting for transfers between devices  353 us (76%)
  starting transfers between devices  46.4 us (10%)
  local copies, waits for them, and re-layouts  26.1 us (6%)
  other arithmetic  15.9 us (3%)
  between operations  14.2 us (3%)
  matrix products  5.83 us (1%)
    reduce_scatter x1, waiting for transfers between devices, local(): lax.psum_scatter(accum.reshape(HEAD_BLOCK_LIMIT * PRUNE_BLOCK_ROWS, HEAD_...  206 us
    all_gather x1, waiting for transfers between devices, local(): gathered_w = lax.all_gather(key_block_matrix, 'dp', axis=1, tiled=True)  84.5 us
    all_to_all x2, waiting for transfers between devices, local(): lax.all_to_all(partial_value, 'tensor', split_axis=0, concat_axis=1, tile...  32.8 us
    all_to_all x2, waiting for transfers between devices, local(): group_x = jnp.concatenate(lax.all_to_all(sent, 'tensor', 0, 0), axis=0)  29.1 us
    all_to_all x2, starting transfers between devices, local(): group_x = jnp.concatenate(lax.all_to_all(sent, 'tensor', 0, 0), axis=0)  28.5 us
    all_to_all x2, starting transfers between devices, local(): lax.all_to_all(partial_value, 'tensor', split_axis=0, concat_axis=1, tile...  17.9 us
    reshape x2, other arithmetic, local(): partial_value.reshape(grads_here.shape[0], 1, HEAD_BLOCK_LIMIT * PRUNE_BL...  11.6 us
    reshape x3, local copies, waits for them, and re-layouts, local(): partial_value.reshape(grads_here.shape[0], 1, HEAD_BLOCK_LIMIT * PRUNE_BL...  9.4 us
  transfers between devices with their start and end apart: 6, of which 6 were waited for; matrix products, arithmetic and copies ran while one was open for 10% of the time, Pallas kernels for 0%

profile of v1, /device:TPU:6, one launch (start us, length us, event | category | flops | bytes accessed | tf_op | source)
XLA Modules:
  0.0 461.4 jit_solution(7894493445154762259)
XLA Ops:
  7.2 1.0 slice_bitcast_fusion
  8.2 1.0 stack.12
  9.2 13.2 %all-to-all-start.1 = ((bf16[8,8,8192]{2,1,0:T(8,128)(2,1)}), bf16[8,8,8192]{2,1,0:T(8,128)(2,1)S(1)}, u32[]{:S(2)}, u32[]{:S(2)}) async-start(bf16[8,8,8192]{2,1,0:T(8,128)(2,1)} %stack.12), calls=%async_computation.1 | async-start | bytes 2097152 | tf_op jit(solution)/shard_map/all_to_all | solution.py:32
  22.4 0.7 all-gather.2.cloned.1.call-update
  23.1 16.4 %all-to-all-done.1 = bf16[8,8,8192]{2,1,0:T(8,128)(2,1)S(1)} async-done(((bf16[8,8,8192]{2,1,0:T(8,128)(2,1)}), bf16[8,8,8192]{2,1,0:T(8,128)(2,1)S(1)}, u32[]{:S(2)}, u32[]{:S(2)}) %all-to-all-start.1) | async-done | bytes 1048608 | tf_op jit(solution)/shard_map/all_to_all | solution.py:32
  39.5 1.0 stack.11
  40.6 15.3 %all-to-all-start = ((bf16[8,8,8192]{2,1,0:T(8,128)(2,1)}), bf16[8,8,8192]{2,1,0:T(8,128)(2,1)S(1)}, u32[]{:S(2)}, u32[]{:S(2)}) async-start(bf16[8,8,8192]{2,1,0:T(8,128)(2,1)} %stack.11), calls=%async_computation | async-start | bytes 2097152 | tf_op jit(solution)/shard_map/all_to_all | solution.py:32
  56.9 12.7 %all-to-all-done = bf16[8,8,8192]{2,1,0:T(8,128)(2,1)S(1)} async-done(((bf16[8,8,8192]{2,1,0:T(8,128)(2,1)}), bf16[8,8,8192]{2,1,0:T(8,128)(2,1)S(1)}, u32[]{:S(2)}, u32[]{:S(2)}) %all-to-all-start) | async-done | bytes 1048608 | tf_op jit(solution)/shard_map/all_to_all | solution.py:32
  69.8 0.7 copy.16
  70.5 0.7 gather_fusion.1
  71.3 0.7 gather_fusion
  72.0 0.8 fusion.11
  72.8 2.8 add_multiply_fusion
  75.7 84.5 %all-gather.2.cloned.1.call-done = bf16[1,6144,128]{2,1,0:T(8,128)(2,1)} async-done(((bf16[1,96,128]{2,1,0:T(8,128)(2,1)}), bf16[1,6144,128]{2,1,0:T(8,128)(2,1)}) %all-gather.2.cloned.1.call-update) | async-done | bytes 1572880 | tf_op jit(solution)/shard_map/all_gather | solution.py:21
  160.2 2.1 broadcast_multiply_fusion
  163.0 1.4 copy.21
  164.4 4.4 reshape.114
  169.4 6.2 %reduce = bf16[64,6144]{1,0:T(8,128)(2,1)} reduce(bf16[64,1,6144]{2,1,0:T(2,128)(2,1)S(1)} %reshape.114, bf16[]{:T(256)} %broadcast.60), dimensions={1}, to_apply=%reshape.114.reduce_sub_computation | reduce | bytes 1572866 | tf_op jit(solution)/shard_map/reshape | solution.py:41
  175.6 3.2 reshape.116
  178.8 13.1 %all-to-all-start.3 = ((bf16[8,2,24576]{2,1,0:T(2,128)(2,1)}), bf16[8,2,24576]{2,1,0:T(2,128)(2,1)S(1)}, u32[]{:S(2)}, u32[]{:S(2)}) async-start(bf16[8,2,24576]{2,1,0:T(2,128)(2,1)} %reshape.116), calls=%async_computation.4 | async-start | bytes 1572864 | tf_op jit(solution)/shard_map/all_to_all | solution.py:44
  192.5 1.4 copy.18
  193.9 4.4 reshape.112
  198.4 5.4 %reduce.1 = bf16[64,6144]{1,0:T(8,128)(2,1)S(1)} reduce(bf16[64,1,6144]{2,1,0:T(2,128)(2,1)S(1)} %reshape.112, bf16[]{:T(256)} %broadcast.60), dimensions={1}, to_apply=%reshape.112.reduce_sub_computation | reduce | bytes 1572866 | tf_op jit(solution)/shard_map/reshape | solution.py:41
  203.7 1.7 reshape.118
  205.4 10.2 %all-to-all-done.3 = bf16[8,2,24576]{2,1,0:T(2,128)(2,1)S(1)} async-done(((bf16[8,2,24576]{2,1,0:T(2,128)(2,1)}), bf16[8,2,24576]{2,1,0:T(2,128)(2,1)S(1)}, u32[]{:S(2)}, u32[]{:S(2)}) %all-to-all-start.3) | async-done | bytes 786464 | tf_op jit(solution)/shard_map/all_to_all | solution.py:44
  215.6 4.8 %all-to-all-start.2 = ((bf16[8,2,24576]{2,1,0:T(2,128)(2,1)}), bf16[8,2,24576]{2,1,0:T(2,128)(2,1)S(1)}, u32[]{:S(2)}, u32[]{:S(2)}) async-start(bf16[8,2,24576]{2,1,0:T(2,128)(2,1)} %reshape.118), calls=%async_computation.3 | async-start | bytes 1572864 | tf_op jit(solution)/shard_map/all_to_all | solution.py:44
  220.4 0.8 reshape.117
  222.2 22.6 %all-to-all-done.2 = bf16[8,2,24576]{2,1,0:T(2,128)(2,1)S(1)} async-done(((bf16[8,2,24576]{2,1,0:T(2,128)(2,1)}), bf16[8,2,24576]{2,1,0:T(2,128)(2,1)S(1)}, u32[]{:S(2)}, u32[]{:S(2)}) %all-to-all-start.2) | async-done | bytes 786464 | tf_op jit(solution)/shard_map/all_to_all | solution.py:44
  244.8 0.8 reshape.119
  246.6 0.7 pad_maximum_fusion
  247.3 205.8 %reduce-scatter.2.cloned.1.call-done = f32[96,128]{1,0:T(8,128)} async-done(((f32[6144,128]{1,0:T(8,128)}), f32[96,128]{1,0:T(8,128)}) %reduce-scatter.2.cloned.1.call-update) | async-done | bytes 49168 | tf_op jit(solution)/shard_map/reduce_scatter | solution.py:49
  453.1 1.4 multiply_bitcast_fusion
  (23 shorter events, 5.1 us)
Async XLA Ops:
  9.2 30.3 %all-to-all-start.1 = ((bf16[8,8,8192]{2,1,0:T(8,128)(2,1)}), bf16[8,8,8192]{2,1,0:T(8,128)(2,1)S(1)}, u32[]{:S(2)}, u32[]{:S(2)}) async-start(bf16[8,8,8192]{2,1,0:T(8,128)(2,1)} %stack.12), calls=%async_computation.1 | async-start | bytes 2097152 | tf_op jit(solution)/shard_map/all_to_all | solution.py:32
  22.4 137.8 %all-gather.2.cloned.1.call-start = ((), (), s32[]{:S(2)}) async-start(), calls=%async_computation.6 | async-start | bytes 1597440 | tf_op jit(solution)/shard_map/all_gather | solution.py:21
  39.5 16.3 %copy-start.1 = (s32[8,48]{1,0:T(8,128)S(1)}, s32[8,48]{1,0:T(8,128)}, u32[]{:S(2)}) copy-start(s32[8,48]{1,0:T(8,128)} %param.9) | copy-start | bytes 4612
  40.6 29.0 %all-to-all-start = ((bf16[8,8,8192]{2,1,0:T(8,128)(2,1)}), bf16[8,8,8192]{2,1,0:T(8,128)(2,1)S(1)}, u32[]{:S(2)}, u32[]{:S(2)}) async-start(bf16[8,8,8192]{2,1,0:T(8,128)(2,1)} %stack.11), calls=%async_computation | async-start | bytes 2097152 | tf_op jit(solution)/shard_map/all_to_all | solution.py:32
  55.9 397.2 %reduce-scatter.2.cloned.1.call-start = ((), (), s32[]{:S(2)}) async-start(), calls=%async_computation.5 | async-start | bytes 3194880 | tf_op jit(solution)/shard_map/reduce_scatter | solution.py:49
  70.5 1.4 copy-start
  178.8 36.9 %all-to-all-start.3 = ((bf16[8,2,24576]{2,1,0:T(2,128)(2,1)}), bf16[8,2,24576]{2,1,0:T(2,128)(2,1)S(1)}, u32[]{:S(2)}, u32[]{:S(2)}) async-start(bf16[8,2,24576]{2,1,0:T(2,128)(2,1)} %reshape.116), calls=%async_computation.4 | async-start | bytes 1572864 | tf_op jit(solution)/shard_map/all_to_all | solution.py:44
  215.6 29.2 %all-to-all-start.2 = ((bf16[8,2,24576]{2,1,0:T(2,128)(2,1)}), bf16[8,2,24576]{2,1,0:T(2,128)(2,1)S(1)}, u32[]{:S(2)}, u32[]{:S(2)}) async-start(bf16[8,2,24576]{2,1,0:T(2,128)(2,1)} %reshape.118), calls=%async_computation.3 | async-start | bytes 1572864 | tf_op jit(solution)/shard_map/all_to_all | solution.py:44
Sparse Core Ops, SparseCore 0:
  25.4 134.7 all-gather.1
  163.0 290.0 reduce-scatter.1
